TPU v7x, 128 devices: a whole 4x4x4 slice. The times are simulated.
128 devices in a mesh: row: 16 (over y, x), col: 8 (over z, core).
Axes of the slice: x: 4, y: 4, z: 4, core: 2. Of those that a mesh axis runs over, the one named last changes fastest.
Arguments:
- tokens: bfloat16 [16384, 1280], P(('row', 'col')), may hold values from -6 to 6
- image_sizes: int32 [16, 8], replicated, may hold values from 1 to 48, 256 in all within a row
- slot_of: int32 [128], replicated, may hold values from 0 to 127, as said below
- ln_gain: float32 [1, 2, 1280], replicated, may hold values from 0.25 to 1.75
- ln_bias: float32 [1, 2, 1280], replicated, may hold values from -3 to 3
- w_qkv: bfloat16 [1, 1280, 3840], P(None, 'row', 'col')
- w_out: bfloat16 [1, 1280, 1280], P(None, 'col', 'row'), may hold values from -0.15625 to 0.15625
- w_up: bfloat16 [1, 1280, 5120], P(None, 'row', 'col'), may hold values from -0.15625 to 0.15625
- w_down: bfloat16 [1, 5120, 1280], P(None, 'col', 'row'), may hold values from -0.078125 to 0.078125
- merge_gain: float32 [1280], replicated, may hold values from 0.25 to 1.75
- merge_bias: float32 [1280], replicated, may hold values from -3 to 3
- w_merge: bfloat16 [5120, 4096], P('row', 'col'), may hold values from -0.078125 to 0.078125
Outputs:
- merged_out: bfloat16 [6144, 4096], P('row', 'col')
- req_norm: float32 [128], P('row')
- req_max: float32 [128], P('row')
Inputs may be any that keep to these rules, and one draw needn't show every extreme that they name: Each row of image_sizes sums to 256 and holds 48 at least once. A permutation of the slots. Request g * 8 + j goes to the row group slot_of // 8, which holds 8 slots. No row group sends more than one request to any row group.
All inputs are finite; a program needn't handle non-finite values.
Results may differ from a plain program's by a relative error of at most 0.018.
The roundings to bfloat16 on the way count: a program that leaves them out, or rounds other values in their place, can miss the bound.
Values may be sent and summed in bfloat16 or wider, within the bound.
A program may use at most 64 MiB of HBM per device.

v0:
```python
import jax
import jax.numpy as jnp
from jax import lax
from jax.sharding import PartitionSpec as P

D = 1280
HEAD_DIM = 80
OUT = 4096
IMG_ROW = 8


def layer_norm(values, gain, bias):
    center = jnp.mean(values, axis=-1, keepdims=True)
    shifted = values - center
    spread = jnp.mean(shifted * shifted, axis=-1, keepdims=True)
    return shifted * lax.rsqrt(spread + 1e-06) * gain + bias


def segment_ids(sizes_row, count):
    bounds = jnp.cumsum(sizes_row)
    merged_index = jnp.arange(count, dtype=jnp.int32) // 4
    return jnp.sum((merged_index[:, None] >= bounds[None, :]).astype(jnp.int32), axis=1)


def attend(qkv, segments):
    count = qkv.shape[0]
    width = min(512, count)
    query = qkv[:, :, 0]
    keys = qkv[:, :, 1]
    values = qkv[:, :, 2]
    results = []
    for offset in range(0, count, width):
        scores = jnp.einsum(
            "qhd,khd->hqk", query[offset : offset + width], keys, preferred_element_type=jnp.float32
        ) * HEAD_DIM ** (-0.5)
        same = segments[offset : offset + width, None] == segments[None, :]
        scores = jnp.where(same[None], scores, -1e30)
        peak = jnp.max(scores, axis=-1, keepdims=True)
        expo = jnp.exp(scores - peak)
        weights = (expo / jnp.sum(expo, axis=-1, keepdims=True)).astype(jnp.bfloat16)
        context = jnp.einsum("hqk,khd->qhd", weights, values, preferred_element_type=jnp.float32)
        results.append(context.astype(jnp.bfloat16).reshape(width, -1))
    return jnp.concatenate(results, axis=0)


def local(
    tokens,
    image_sizes,
    slot_of,
    ln_gain,
    ln_bias,
    w_qkv,
    w_out,
    w_up,
    w_down,
    merge_gain,
    merge_bias,
    w_merge,
):
    n_col = lax.axis_size("col")
    row_index = lax.axis_index("row")
    tok_dev = tokens.shape[0]
    tok_row = tok_dev * n_col
    merged_row = tok_row // 4
    most = merged_row * 3 // 16
    sizes_here = lax.dynamic_index_in_dim(image_sizes, row_index, 0, keepdims=False)
    segments = segment_ids(sizes_here, tok_row)
    stream = tokens
    normed = layer_norm(stream.astype(jnp.float32), ln_gain[0, 0], ln_bias[0, 0]).astype(
        jnp.bfloat16
    )
    normed_all = lax.all_gather(normed, "col", axis=0, tiled=True)
    left_part = normed_all
    qkv = jnp.dot(
        left_part,
        lax.all_gather(w_qkv[0], "row", axis=0, tiled=True),
        preferred_element_type=jnp.float32,
    )
    qkv = qkv.astype(jnp.bfloat16).reshape(tok_row, -1, 3, HEAD_DIM)
    context = attend(qkv, segments)
    attn_terms = jnp.dot(
        context,
        lax.all_gather(w_out[0], "row", axis=1, tiled=True),
        preferred_element_type=jnp.float32,
    )
    attn_out = lax.psum_scatter(
        attn_terms.astype(jnp.bfloat16), "col", scatter_dimension=0, tiled=True
    ).astype(jnp.float32)
    stream = (stream.astype(jnp.float32) + attn_out).astype(jnp.bfloat16)
    normed = layer_norm(stream.astype(jnp.float32), ln_gain[0, 1], ln_bias[0, 1]).astype(
        jnp.bfloat16
    )
    normed_mlp = lax.all_gather(normed, "col", axis=0, tiled=True)
    left_part = normed_mlp
    up_value = jnp.dot(
        left_part,
        lax.all_gather(w_up[0], "row", axis=0, tiled=True),
        preferred_element_type=jnp.float32,
    )
    hidden = jax.nn.gelu(up_value, approximate=False).astype(jnp.bfloat16)
    mlp_terms = jnp.dot(
        hidden,
        lax.all_gather(w_down[0], "row", axis=1, tiled=True),
        preferred_element_type=jnp.float32,
    )
    mlp_out = lax.psum_scatter(
        mlp_terms.astype(jnp.bfloat16), "col", scatter_dimension=0, tiled=True
    ).astype(jnp.float32)
    stream = (stream.astype(jnp.float32) + mlp_out).astype(jnp.bfloat16)
    merged = layer_norm(stream.astype(jnp.float32), merge_gain, merge_bias).astype(jnp.bfloat16)
    merged = merged.reshape(tok_dev // 4, 4 * D)
    merged_all = lax.all_gather(merged, "col", axis=0, tiled=True)
    out_dev = w_merge.shape[1]
    left_part = merged_all
    projected = jnp.dot(
        left_part,
        lax.all_gather(w_merge, "row", axis=0, tiled=True),
        preferred_element_type=jnp.float32,
    ).astype(jnp.bfloat16)
    reqs = slot_of.shape[0]
    numbers = jnp.arange(reqs, dtype=jnp.int32)
    req_at_slot = jnp.sum(
        jnp.where(slot_of[None, :] == numbers[:, None], numbers[None, :], 0), axis=1
    )
    starts = jnp.cumsum(image_sizes, axis=1) - image_sizes
    starts_flat = starts.reshape(-1)
    sizes_flat = image_sizes.reshape(-1)
    inner = jnp.arange(most, dtype=jnp.int32)
    request = lax.dynamic_slice_in_dim(req_at_slot, row_index * IMG_ROW, IMG_ROW)
    group = request // IMG_ROW
    source = ((group * merged_row + starts_flat[request])[:, None] + inner[None, :]).reshape(-1)
    valid = (inner[None, :] < sizes_flat[request][:, None]).reshape(-1)
    rows_init = jnp.zeros((IMG_ROW * most, out_dev), jnp.bfloat16)
    piece = lax.all_gather(projected, "row", axis=0, tiled=True)
    inside = valid & (source >= 0) & (source < piece.shape[0])
    taken = jnp.take(piece, jnp.clip(source, 0, piece.shape[0] - 1), axis=0)
    placed = jnp.where(inside[:, None], taken, rows_init)
    blocks = placed.astype(jnp.float32).reshape(IMG_ROW, most, out_dev)
    squares = jnp.sum(blocks * blocks, axis=(1, 2))
    peaks = jnp.max(jnp.abs(blocks), axis=(1, 2))
    squares = lax.psum(squares, "col")
    peaks = lax.pmax(peaks, "col")
    slot_size = sizes_flat[request].astype(jnp.float32)
    req_norm = jnp.sqrt(squares / (slot_size * OUT) + 1e-06)
    merged_out = (
        (blocks / req_norm[:, None, None]).astype(jnp.bfloat16).reshape(IMG_ROW * most, out_dev)
    )
    return (merged_out, req_norm, peaks)


def solution(mesh):
    in_specs = (
        P(("row", "col"), None),
        P(),
        P(),
        P(),
        P(),
        P(None, "row", "col"),
        P(None, "col", "row"),
        P(None, "row", "col"),
        P(None, "col", "row"),
        P(),
        P(),
        P("row", "col"),
    )
    out_specs = (P("row", "col"), P("row"), P("row"))
    return jax.shard_map(local, mesh=mesh, in_specs=in_specs, out_specs=out_specs, check_vma=False)
```

profile of v0, /device:TPU:1, one launch (start us, length us, event | category | flops | bytes accessed | tf_op | source)
XLA Modules:
  0.0 487.1 jit_solution(6885048592995645499)
XLA Ops:
  9.9 1.2 fusion.45
  11.1 2.0 fusion.48
  15.1 22.5 %all-gather.1 = bf16[1,160,1280]{1,0,2:T(2,128)(2,1)S(1)} all-gather(bf16[1,160,80]{1,0,2:T(2,128)(2,1)S(1)} %copy.48), channel_id=3, replica_groups=mesh['row'=16,'col'=8] {'row'}, dimensions={2}, use_global_device_ids=true | all-gather | bytes 435200 | tf_op jit(solution)/shard_map/all_gather | solution.py:83
  37.6 1.8 copy.49
  40.2 14.8 %all-gather.23.cloned.1.call-done = bf16[1,1280,480]{2,1,0:T(8,128)(2,1)} async-done(((bf16[1,80,480]{2,1,0:T(8,128)(2,1)}), bf16[1,1280,480]{2,1,0:T(8,128)(2,1)}) %all-gather.23.cloned.1.call-update) | async-done | bytes 1228816 | tf_op jit(solution)/shard_map/all_gather | solution.py:76
  55.0 30.0 %all-gather.13.cloned.1.call-done = bf16[1024,1280]{1,0:T(8,128)(2,1)} async-done(((bf16[128,1280]{1,0:T(8,128)(2,1)}), bf16[1024,1280]{1,0:T(8,128)(2,1)}) %all-gather.13.cloned.1.call-update) | async-done | bytes 2621456 | tf_op jit(solution)/shard_map/all_gather | solution.py:72
  85.1 3.6 convolution_convert_fusion.2
  88.6 3.7 fusion.112
  92.3 3.6 fusion.111
  95.9 3.2 fusion.31
  100.2 2.4 convolution_convert_fusion.1
  103.9 31.0 %reduce-scatter.3.cloned.1.call-done = bf16[128,1280]{1,0:T(8,128)(2,1)} async-done(((bf16[1024,1280]{1,0:T(8,128)(2,1)}), bf16[128,1280]{1,0:T(8,128)(2,1)}) %reduce-scatter.3.cloned.1.call-update) | async-done | bytes 327696 | tf_op jit(solution)/shard_map/reduce_scatter | solution.py:86
  137.5 43.5 %all-gather.25.cloned.1.call-done = bf16[1,1280,640]{2,1,0:T(8,128)(2,1)} async-done(((bf16[1,80,640]{2,1,0:T(8,128)(2,1)}), bf16[1,1280,640]{2,1,0:T(8,128)(2,1)}) %all-gather.25.cloned.1.call-update) | async-done | bytes 1638416 | tf_op jit(solution)/shard_map/all_gather | solution.py:97
  181.0 45.1 %all-gather.27.cloned.1.call-done = bf16[1,640,1280]{1,2,0:T(8,128)(2,1)} async-done(((bf16[1,640,80]{1,2,0:T(8,128)(2,1)}), bf16[1,640,1280]{1,2,0:T(8,128)(2,1)}) %all-gather.27.cloned.1.call-update) | async-done | bytes 1638416 | tf_op jit(solution)/shard_map/all_gather | solution.py:103
  226.1 29.3 %all-gather.15.cloned.1.call-done = bf16[1024,1280]{1,0:T(8,128)(2,1)} async-done(((bf16[128,1280]{1,0:T(8,128)(2,1)}), bf16[1024,1280]{1,0:T(8,128)(2,1)}) %all-gather.15.cloned.1.call-update) | async-done | bytes 2621456 | tf_op jit(solution)/shard_map/all_gather | solution.py:93
  255.3 13.0 %convolution_convert_fusion = bf16[1024,1280]{1,0:T(8,128)(2,1)} fusion(bf16[1,640,1280]{1,2,0:T(8,128)(2,1)} %all-gather.27.cloned.1.call-done, bf16[1024,1280]{1,0:T(8,128)(2,1)} %all-gather.15.cloned.1.call-done, bf16[1,1280,640]{2,1,0:T(8,128)(2,1)} %all-gather.25.cloned.1.call-done), kind=kOutput, calls=%fused_computation.12 | convolution fusion | flops 3399352320 | bytes 8519680 | tf_op jit(solution)/shard_map/dot_general | solution.py:101
  269.2 31.4 %reduce-scatter.5.cloned.1.call-done = bf16[128,1280]{1,0:T(8,128)(2,1)} async-done(((bf16[1024,1280]{1,0:T(8,128)(2,1)}), bf16[128,1280]{1,0:T(8,128)(2,1)}) %reduce-scatter.5.cloned.1.call-update) | async-done | bytes 327696 | tf_op jit(solution)/shard_map/reduce_scatter | solution.py:106
  305.1 55.3 %all-gather.19.cloned.1.call-done = bf16[5120,512]{1,0:T(8,128)(2,1)} async-done(((bf16[320,512]{1,0:T(8,128)(2,1)}), bf16[5120,512]{1,0:T(8,128)(2,1)}) %all-gather.19.cloned.1.call-update) | async-done | bytes 5242896 | tf_op jit(solution)/shard_map/all_gather | solution.py:117
  360.4 28.6 %all-gather.17.cloned.1.call-done = bf16[256,5120]{1,0:T(8,128)(2,1)} async-done(((bf16[32,5120]{1,0:T(8,128)(2,1)}), bf16[256,5120]{1,0:T(8,128)(2,1)}) %all-gather.17.cloned.1.call-update) | async-done | bytes 2621456 | tf_op jit(solution)/shard_map/all_gather | solution.py:112
  389.0 5.5 %convolution_convert_fusion.3 = bf16[256,512]{1,0:T(8,128)(2,1)} fusion(bf16[256,5120]{1,0:T(8,128)(2,1)} %all-gather.17.cloned.1.call-done, bf16[5120,512]{1,0:T(8,128)(2,1)} %all-gather.19.cloned.1.call-done), kind=kOutput, calls=%fused_computation.47 | convolution fusion | flops 1342308352 | bytes 8126464 | tf_op jit(solution)/shard_map/dot_general | solution.py:115
  397.0 48.9 %all-gather.21.cloned.1.call-done = bf16[4096,512]{1,0:T(8,128)(2,1)} async-done(((bf16[256,512]{1,0:T(8,128)(2,1)}), bf16[4096,512]{1,0:T(8,128)(2,1)}) %all-gather.21.cloned.1.call-update) | async-done | bytes 4194320 | tf_op jit(solution)/shard_map/all_gather | solution.py:134
  445.8 4.8 gather_fusion.2
  451.2 12.7 %psum.7 = f32[8]{0:T(128)S(1)} all-reduce(f32[8]{0:T(128)S(1)} %reduce_sum.118), channel_id=1, replica_groups=mesh['row'=16,'col'=8] {'col'}, use_global_device_ids=true, to_apply=%region_18.19 | all-reduce | flops 8 | bytes 64 | tf_op jit(solution)/shard_map/psum | solution.py:141
  464.3 15.0 %pmax.7 = f32[8]{0:T(128)} all-reduce(f32[8]{0:T(128)S(1)} %reduce_max.38), channel_id=1, replica_groups=mesh['row'=16,'col'=8] {'col'}, use_global_device_ids=true, to_apply=%region_21.22 | all-reduce | flops 8 | bytes 64 | tf_op jit(solution)/shard_map/pmax | solution.py:142
  (86 shorter events, 20.0 us)
Async XLA Ops:
  7.2 47.9 %all-gather.23.cloned.1.call-start = ((), (), s32[]{:S(2)}) async-start(), calls=%async_computation.9 | async-start | bytes 1392640 | tf_op jit(solution)/shard_map/all_gather | solution.py:76
  7.9 77.2 %all-gather.13.cloned.1.call-start = ((), (), s32[]{:S(2)}) async-start(), calls=%async_computation.2 | async-start | bytes 2949120 | tf_op jit(solution)/shard_map/all_gather | solution.py:72
  13.1 121.8 %reduce-scatter.3.cloned.1.call-start = ((), (), s32[]{:S(2)}) async-start(), calls=%async_computation.3 | async-start | bytes 2949120 | tf_op jit(solution)/shard_map/reduce_scatter | solution.py:86
  95.9 3.4 copy-start.6
  100.2 34.7 %copy-start = (bf16[128,1280]{1,0:T(8,128)(2,1)S(1)}, bf16[128,1280]{1,0:T(8,128)(2,1)}, u32[]{:S(2)}) copy-start(bf16[128,1280]{1,0:T(8,128)(2,1)} %param.12) | copy-start | bytes 983044
  102.7 78.3 %all-gather.25.cloned.1.call-start = ((), (), s32[]{:S(2)}) async-start(), calls=%async_computation.10 | async-start | bytes 1740800 | tf_op jit(solution)/shard_map/all_gather | solution.py:97
  103.3 122.8 %all-gather.27.cloned.1.call-start = ((), (), s32[]{:S(2)}) async-start(), calls=%async_computation.11 | async-start | bytes 1740800 | tf_op jit(solution)/shard_map/all_gather | solution.py:103
  103.8 151.5 %all-gather.15.cloned.1.call-start = ((), (), s32[]{:S(2)}) async-start(), calls=%async_computation.4 | async-start | bytes 2949120 | tf_op jit(solution)/shard_map/all_gather | solution.py:93
  137.3 163.3 %reduce-scatter.5.cloned.1.call-start = ((), (), s32[]{:S(2)}) async-start(), calls=%async_computation.5 | async-start | bytes 2949120 | tf_op jit(solution)/shard_map/reduce_scatter | solution.py:106
  268.3 34.6 %copy-start.2 = (f32[1280]{0:T(1024)S(1)}, f32[1280]{0:T(1024)}, u32[]{:S(2)}) copy-start(f32[1280]{0:T(1024)} %param.22) | copy-start | bytes 15364
  268.3 34.6 %copy-start.3 = (f32[1280]{0:T(1024)S(1)}, f32[1280]{0:T(1024)}, u32[]{:S(2)}) copy-start(f32[1280]{0:T(1024)} %param.21) | copy-start | bytes 15364
  268.4 92.0 %all-gather.19.cloned.1.call-start = ((), (), s32[]{:S(2)}) async-start(), calls=%async_computation.7 | async-start | bytes 5570560 | tf_op jit(solution)/shard_map/all_gather | solution.py:117
  269.1 119.9 %all-gather.17.cloned.1.call-start = ((), (), s32[]{:S(2)}) async-start(), calls=%async_computation.6 | async-start | bytes 2949120 | tf_op jit(solution)/shard_map/all_gather | solution.py:112
  305.1 89.5 %copy-start.1 = (s32[16,8]{0,1:T(8,128)S(1)}, s32[16,8]{0,1:T(8,128)}, u32[]{:S(2)}) copy-start(s32[16,8]{0,1:T(8,128)} %param.13) | copy-start | bytes 1540
  305.1 89.7 %copy-start.5 = (s32[128]{0:T(128)S(1)}, s32[128]{0:T(128)}, u32[]{:S(2)}) copy-start(s32[128]{0:T(128)} %param.14) | copy-start | bytes 1540
  305.1 140.7 %all-gather.21.cloned.1.call-start = ((), (), s32[]{:S(2)}) async-start(), calls=%async_computation.8 | async-start | bytes 4456448 | tf_op jit(solution)/shard_map/all_gather | solution.py:134
  464.0 16.3 %copy-start.4 = (f32[8]{0:T(128)}, f32[8]{0:T(128)S(1)}, u32[]{:S(2)}) copy-start(f32[8]{0:T(128)S(1)} %add_sqrt_fusion) | copy-start | bytes 100
Sparse Core Ops, SparseCore 0:
  10.1 44.8 all-gather.22
  57.3 27.7 all-gather.12
  102.8 32.0 reduce-scatter.2
  136.9 44.0 all-gather.24
  183.0 43.0 all-gather.26
  228.2 27.1 all-gather.14
  268.5 32.0 reduce-scatter.4
  302.7 57.6 all-gather.18
  362.7 26.2 all-gather.16
  394.7 51.1 all-gather.20
where the time goes:
time: 488 us; the launch traced here: 487 us
  waiting for transfers between devices  360 us (74%)
  blocking collectives  50.3 us (10%)
  matrix products  35.8 us (7%)
  between operations  14.4 us (3%)
  other arithmetic  13.2 us (3%)
  local copies, waits for them, and re-layouts  12.6 us (3%)
    all_gather x1, waiting for transfers between devices, local(): lax.all_gather(w_merge, 'row', axis=0, tiled=True)  55.3 us
    all_gather x1, waiting for transfers between devices, local(): piece = lax.all_gather(projected, 'row', axis=0, tiled=True)  48.9 us
    all_gather x1, waiting for transfers between devices, local(): lax.all_gather(w_down[0], 'row', axis=1, tiled=True)  45.1 us
    all_gather x1, waiting for transfers between devices, local(): lax.all_gather(w_up[0], 'row', axis=0, tiled=True)  43.5 us
    reduce_scatter x1, waiting for transfers between devices, local(): lax.psum_scatter(mlp_terms.astype(jnp.bfloat16), 'col', scatter_dimension...  31.4 us
    reduce_scatter x1, waiting for transfers between devices, local(): lax.psum_scatter(attn_terms.astype(jnp.bfloat16), 'col', scatter_dimensio...  31 us
    all_gather x1, waiting for transfers between devices, local(): normed_all = lax.all_gather(normed, 'col', axis=0, tiled=True)  30 us
    all_gather x1, waiting for transfers between devices, local(): normed_mlp = lax.all_gather(normed, 'col', axis=0, tiled=True)  29.3 us
  transfers between devices with their start and end apart: 10, of which 10 were waited for; matrix products, arithmetic and copies ran while one was open for 4% of the time, Pallas kernels for 0%

commit v1 on v0

--- a/solution.py
+++ b/solution.py
@@ -138,7 +138,9 @@
     blocks = placed.astype(jnp.float32).reshape(IMG_ROW, most, out_dev)
     squares = jnp.sum(blocks * blocks, axis=(1, 2))
     peaks = jnp.max(jnp.abs(blocks), axis=(1, 2))
-    squares = lax.psum(squares, "col")
+    squares = squares
+    for hop in (1, 2, 4):
+        squares = squares + lax.ppermute(squares, "col", [(dev, dev ^ hop) for dev in range(8)])
     peaks = lax.pmax(peaks, "col")
     slot_size = sizes_flat[request].astype(jnp.float32)
     req_norm = jnp.sqrt(squares / (slot_size * OUT) + 1e-06)

time: 488 us -> 484 us (level)
  blocking collectives: 50.3 us -> 34.9 us
  waiting for transfers between devices: 360 us -> 365 us
    psum x1 -> x0, blocking collectives: 12.7 us -> none  [local(): squares = lax.psum(squares, 'col')]
  transfers between devices with their start and end apart: 10 -> 13, of which waited for: 10 -> 12; matrix products, arithmetic and copies ran while one was open for 4% -> 4% of each run, Pallas kernels for 0% -> 0%
where the time goes in v1:
time: 484 us; the launch traced here: 479 us
  waiting for transfers between devices  365 us (75%)
  matrix products  35.8 us (7%)
  blocking collectives  34.9 us (7%)
  between operations  14.4 us (3%)
  other arithmetic  13.2 us (3%)
  local copies, waits for them, and re-layouts  12.6 us (3%)
    all_gather x1, waiting for transfers between devices, local(): lax.all_gather(w_merge, 'row', axis=0, tiled=True)  55.3 us
    all_gather x1, waiting for transfers between devices, local(): piece = lax.all_gather(projected, 'row', axis=0, tiled=True)  48.9 us
    all_gather x1, waiting for transfers between devices, local(): lax.all_gather(w_down[0], 'row', axis=1, tiled=True)  45.1 us
    all_gather x1, waiting for transfers between devices, local(): lax.all_gather(w_up[0], 'row', axis=0, tiled=True)  43.5 us
    reduce_scatter x1, waiting for transfers between devices, local(): lax.psum_scatter(mlp_terms.astype(jnp.bfloat16), 'col', scatter_dimension...  31.4 us
    reduce_scatter x1, waiting for transfers between devices, local(): lax.psum_scatter(attn_terms.astype(jnp.bfloat16), 'col', scatter_dimensio...  31 us
    all_gather x1, waiting for transfers between devices, local(): normed_all = lax.all_gather(normed, 'col', axis=0, tiled=True)  30 us
    all_gather x1, waiting for transfers between devices, local(): normed_mlp = lax.all_gather(normed, 'col', axis=0, tiled=True)  29.3 us
  transfers between devices with their start and end apart: 13, of which 12 were waited for; matrix products, arithmetic and copies ran while one was open for 4% of the time, Pallas kernels for 0%

profile of v1, /device:TPU:1, one launch (start us, length us, event | category | flops | bytes accessed | tf_op | source)
XLA Modules:
  0.0 479.2 jit_solution(11447357587388283016)
XLA Ops:
  11.1 2.0 fusion.48
  15.1 22.5 %all-gather.1 = bf16[1,160,1280]{1,0,2:T(2,128)(2,1)S(1)} all-gather(bf16[1,160,80]{1,0,2:T(2,128)(2,1)S(1)} %copy.48), channel_id=3, replica_groups=mesh['row'=16,'col'=8] {'row'}, dimensions={2}, use_global_device_ids=true | all-gather | bytes 435200 | tf_op jit(solution)/shard_map/all_gather | solution.py:83
  37.6 1.8 copy.49
  40.2 14.8 %all-gather.23.cloned.1.call-done = bf16[1,1280,480]{2,1,0:T(8,128)(2,1)} async-done(((bf16[1,80,480]{2,1,0:T(8,128)(2,1)}), bf16[1,1280,480]{2,1,0:T(8,128)(2,1)}) %all-gather.23.cloned.1.call-update) | async-done | bytes 1228816 | tf_op jit(solution)/shard_map/all_gather | solution.py:76
  55.0 30.0 %all-gather.13.cloned.1.call-done = bf16[1024,1280]{1,0:T(8,128)(2,1)} async-done(((bf16[128,1280]{1,0:T(8,128)(2,1)}), bf16[1024,1280]{1,0:T(8,128)(2,1)}) %all-gather.13.cloned.1.call-update) | async-done | bytes 2621456 | tf_op jit(solution)/shard_map/all_gather | solution.py:72
  85.1 3.6 convolution_convert_fusion.2
  88.6 3.7 fusion.112
  92.3 3.6 fusion.111
  95.9 3.2 fusion.31
  100.2 2.4 convolution_convert_fusion.1
  103.9 31.0 %reduce-scatter.3.cloned.1.call-done = bf16[128,1280]{1,0:T(8,128)(2,1)} async-done(((bf16[1024,1280]{1,0:T(8,128)(2,1)}), bf16[128,1280]{1,0:T(8,128)(2,1)}) %reduce-scatter.3.cloned.1.call-update) | async-done | bytes 327696 | tf_op jit(solution)/shard_map/reduce_scatter | solution.py:86
  137.5 43.5 %all-gather.25.cloned.1.call-done = bf16[1,1280,640]{2,1,0:T(8,128)(2,1)} async-done(((bf16[1,80,640]{2,1,0:T(8,128)(2,1)}), bf16[1,1280,640]{2,1,0:T(8,128)(2,1)}) %all-gather.25.cloned.1.call-update) | async-done | bytes 1638416 | tf_op jit(solution)/shard_map/all_gather | solution.py:97
  181.0 45.1 %all-gather.27.cloned.1.call-done = bf16[1,640,1280]{1,2,0:T(8,128)(2,1)} async-done(((bf16[1,640,80]{1,2,0:T(8,128)(2,1)}), bf16[1,640,1280]{1,2,0:T(8,128)(2,1)}) %all-gather.27.cloned.1.call-update) | async-done | bytes 1638416 | tf_op jit(solution)/shard_map/all_gather | solution.py:103
  226.1 29.3 %all-gather.15.cloned.1.call-done = bf16[1024,1280]{1,0:T(8,128)(2,1)} async-done(((bf16[128,1280]{1,0:T(8,128)(2,1)}), bf16[1024,1280]{1,0:T(8,128)(2,1)}) %all-gather.15.cloned.1.call-update) | async-done | bytes 2621456 | tf_op jit(solution)/shard_map/all_gather | solution.py:93
  255.3 13.0 %convolution_convert_fusion = bf16[1024,1280]{1,0:T(8,128)(2,1)} fusion(bf16[1,640,1280]{1,2,0:T(8,128)(2,1)} %all-gather.27.cloned.1.call-done, bf16[1024,1280]{1,0:T(8,128)(2,1)} %all-gather.15.cloned.1.call-done, bf16[1,1280,640]{2,1,0:T(8,128)(2,1)} %all-gather.25.cloned.1.call-done), kind=kOutput, calls=%fused_computation.12 | convolution fusion | flops 3399352320 | bytes 8519680 | tf_op jit(solution)/shard_map/dot_general | solution.py:101
  269.2 31.4 %reduce-scatter.5.cloned.1.call-done = bf16[128,1280]{1,0:T(8,128)(2,1)} async-done(((bf16[1024,1280]{1,0:T(8,128)(2,1)}), bf16[128,1280]{1,0:T(8,128)(2,1)}) %reduce-scatter.5.cloned.1.call-update) | async-done | bytes 327696 | tf_op jit(solution)/shard_map/reduce_scatter | solution.py:106
  305.1 55.3 %all-gather.19.cloned.1.call-done = bf16[5120,512]{1,0:T(8,128)(2,1)} async-done(((bf16[320,512]{1,0:T(8,128)(2,1)}), bf16[5120,512]{1,0:T(8,128)(2,1)}) %all-gather.19.cloned.1.call-update) | async-done | bytes 5242896 | tf_op jit(solution)/shard_map/all_gather | solution.py:117
  360.4 28.6 %all-gather.17.cloned.1.call-done = bf16[256,5120]{1,0:T(8,128)(2,1)} async-done(((bf16[32,5120]{1,0:T(8,128)(2,1)}), bf16[256,5120]{1,0:T(8,128)(2,1)}) %all-gather.17.cloned.1.call-update) | async-done | bytes 2621456 | tf_op jit(solution)/shard_map/all_gather | solution.py:112
  389.0 5.5 %convolution_convert_fusion.3 = bf16[256,512]{1,0:T(8,128)(2,1)} fusion(bf16[256,5120]{1,0:T(8,128)(2,1)} %all-gather.17.cloned.1.call-done, bf16[5120,512]{1,0:T(8,128)(2,1)} %all-gather.19.cloned.1.call-done), kind=kOutput, calls=%fused_computation.47 | convolution fusion | flops 1342308352 | bytes 8126464 | tf_op jit(solution)/shard_map/dot_general | solution.py:115
  397.0 48.9 %all-gather.21.cloned.1.call-done = bf16[4096,512]{1,0:T(8,128)(2,1)} async-done(((bf16[256,512]{1,0:T(8,128)(2,1)}), bf16[4096,512]{1,0:T(8,128)(2,1)}) %all-gather.21.cloned.1.call-update) | async-done | bytes 4194320 | tf_op jit(solution)/shard_map/all_gather | solution.py:134
  445.8 4.8 %gather_fusion.2 = bf16[384,512]{1,0:T(8,128)(2,1)S(1)} fusion(bf16[4096,512]{1,0:T(8,128)(2,1)} %all-gather.21.cloned.1.call-done, s32[1024]{0:T(1024)S(1)} %pad_clamp_fusion), kind=kCustom, calls=%fused_computation.2 | custom fusion | bytes 787968 | tf_op jit(solution)/shard_map/jit(_take)/gather | solution.py:136
  452.3 12.4 %pmax.7 = f32[8]{0:T(128)} all-reduce(f32[8]{0:T(128)S(1)} %reduce_max.38), channel_id=1, replica_groups=mesh['row'=16,'col'=8] {'col'}, use_global_device_ids=true, to_apply=%region_20.21 | all-reduce | flops 8 | bytes 64 | tf_op jit(solution)/shard_map/pmax | solution.py:144
  464.8 2.6 collective-permute-done.1
  467.3 2.2 collective-permute-start.2
  (93 shorter events, 23.9 us)
Async XLA Ops:
  7.2 47.9 %all-gather.23.cloned.1.call-start = ((), (), s32[]{:S(2)}) async-start(), calls=%async_computation.9 | async-start | bytes 1392640 | tf_op jit(solution)/shard_map/all_gather | solution.py:76
  7.9 77.2 %all-gather.13.cloned.1.call-start = ((), (), s32[]{:S(2)}) async-start(), calls=%async_computation.2 | async-start | bytes 2949120 | tf_op jit(solution)/shard_map/all_gather | solution.py:72
  13.1 121.8 %reduce-scatter.3.cloned.1.call-start = ((), (), s32[]{:S(2)}) async-start(), calls=%async_computation.3 | async-start | bytes 2949120 | tf_op jit(solution)/shard_map/reduce_scatter | solution.py:86
  95.9 3.4 copy-start.6
  100.2 34.7 %copy-start = (bf16[128,1280]{1,0:T(8,128)(2,1)S(1)}, bf16[128,1280]{1,0:T(8,128)(2,1)}, u32[]{:S(2)}) copy-start(bf16[128,1280]{1,0:T(8,128)(2,1)} %param.12) | copy-start | bytes 983044
  102.7 78.3 %all-gather.25.cloned.1.call-start = ((), (), s32[]{:S(2)}) async-start(), calls=%async_computation.10 | async-start | bytes 1740800 | tf_op jit(solution)/shard_map/all_gather | solution.py:97
  103.3 122.8 %all-gather.27.cloned.1.call-start = ((), (), s32[]{:S(2)}) async-start(), calls=%async_computation.11 | async-start | bytes 1740800 | tf_op jit(solution)/shard_map/all_gather | solution.py:103
  103.8 151.5 %all-gather.15.cloned.1.call-start = ((), (), s32[]{:S(2)}) async-start(), calls=%async_computation.4 | async-start | bytes 2949120 | tf_op jit(solution)/shard_map/all_gather | solution.py:93
  137.3 163.3 %reduce-scatter.5.cloned.1.call-start = ((), (), s32[]{:S(2)}) async-start(), calls=%async_computation.5 | async-start | bytes 2949120 | tf_op jit(solution)/shard_map/reduce_scatter | solution.py:106
  268.3 34.6 %copy-start.2 = (f32[1280]{0:T(1024)S(1)}, f32[1280]{0:T(1024)}, u32[]{:S(2)}) copy-start(f32[1280]{0:T(1024)} %param.22) | copy-start | bytes 15364
  268.3 34.6 %copy-start.3 = (f32[1280]{0:T(1024)S(1)}, f32[1280]{0:T(1024)}, u32[]{:S(2)}) copy-start(f32[1280]{0:T(1024)} %param.21) | copy-start | bytes 15364
  268.4 92.0 %all-gather.19.cloned.1.call-start = ((), (), s32[]{:S(2)}) async-start(), calls=%async_computation.7 | async-start | bytes 5570560 | tf_op jit(solution)/shard_map/all_gather | solution.py:117
  269.1 119.9 %all-gather.17.cloned.1.call-start = ((), (), s32[]{:S(2)}) async-start(), calls=%async_computation.6 | async-start | bytes 2949120 | tf_op jit(solution)/shard_map/all_gather | solution.py:112
  305.1 89.5 %copy-start.1 = (s32[16,8]{0,1:T(8,128)S(1)}, s32[16,8]{0,1:T(8,128)}, u32[]{:S(2)}) copy-start(s32[16,8]{0,1:T(8,128)} %param.13) | copy-start | bytes 1540
  305.1 89.7 %copy-start.5 = (s32[128]{0:T(128)S(1)}, s32[128]{0:T(128)}, u32[]{:S(2)}) copy-start(s32[128]{0:T(128)} %param.14) | copy-start | bytes 1540
  305.1 140.7 %all-gather.21.cloned.1.call-start = ((), (), s32[]{:S(2)}) async-start(), calls=%async_computation.8 | async-start | bytes 4456448 | tf_op jit(solution)/shard_map/all_gather | solution.py:134
  451.4 13.3 %collective-permute-start = (f32[8]{0:T(128)S(1)}, f32[8]{0:T(128)S(1)}, u32[]{:S(2)}, u32[]{:S(2)}) collective-permute-start(f32[8]{0:T(128)S(1)} %reduce_sum.118), channel_id=1, source_target_pairs={{0,1},{1,0},{2,3},{3,2},{4,5},{5,4},{6,7},{7,6},{8,9},{9,8},{10,11... | collective-permute-start | bytes 104 | tf_op jit(solution)/shard_map/ppermute | solution.py:143
  464.7 2.6 collective-permute-start.1
  467.3 3.9 collective-permute-start.2
  471.3 1.1 copy-start.4
Sparse Core Ops, SparseCore 0:
  10.1 44.8 all-gather.22
  57.3 27.7 all-gather.12
  102.8 32.0 reduce-scatter.2
  136.9 44.0 all-gather.24
  183.0 43.0 all-gather.26
  228.2 27.1 all-gather.14
  268.5 32.0 reduce-scatter.4
  302.7 57.6 all-gather.18
  362.7 26.2 all-gather.16
  394.7 51.1 all-gather.20
